TPU v7x, 512 devices: a whole 4x4x16 slice. The times are simulated.
512 devices in a mesh: tile: 64 (over z_lo, y, core), pgroup: 8 (over x, z_hi).
Axes of the slice: x: 4, y: 4, z: 16 (z_hi: 2, z_lo: 8; z = z_hi * 8 + z_lo), core: 2. Of those that a mesh axis runs over, the one named last changes fastest.
Arguments:
- echoes: bfloat16 [32768, 2, 4096], P(('pgroup', 'tile')), may hold values from -6 to 6
- offsets: int32 [64, 32768], P('tile', 'pgroup'), may hold values from 0 to 2041
- phase_index: int32 [64, 32768], P('tile', 'pgroup'), may hold values from 0 to 15
- steering: float32 [2, 64, 32768], P(None, 'tile'), may hold values from -2 to 2
- kernels: float32 [16, 8], replicated, may hold values from -2 to 2
Outputs:
- image: float32 [2, 2048, 16384], P(None, 'pgroup', 'tile')
All inputs are finite; a program needn't handle non-finite values.
Results may differ from a plain program's by a relative error of at most 0.0037.
Values may be sent and summed in bfloat16 or wider, within the bound.
A program may use at most 64 MiB of HBM per device.

v0:
```python
import jax
import jax.numpy as jnp
from jax import lax
from jax.sharding import PartitionSpec as P

ROW_DEV = 256
COL_DEV = 256
STEPS = 4


def passed_along(shard, axis, by):
    length = lax.axis_size(axis)
    return lax.ppermute(shard, axis, [(i, (i + by) % length) for i in range(length)])


def steer_table(rates, curves, columns):
    centred = jnp.arange(columns, dtype=jnp.float32) - (columns - 1) / 2.0
    angle = (
        rates[:, None] * centred[None, :] + curves[:, None] * (centred * centred / columns)[None, :]
    )
    return (jnp.cos(angle).astype(jnp.bfloat16), jnp.sin(angle).astype(jnp.bfloat16))


def shifted_window(pulse_rows, firsts, span):
    length = pulse_rows.shape[2]
    bit_count = max(1, (length - span).bit_length())
    padded_len = span + (1 << bit_count) - 1
    current = jnp.pad(pulse_rows, ((0, 0), (0, 0), (0, max(0, padded_len - length))))
    for level in range(bit_count - 1, -1, -1):
        step_len = 1 << level
        keep = span + step_len - 1
        chosen = (firsts // step_len % 2 == 1)[:, None, None]
        current = jnp.where(chosen, current[:, :, step_len : step_len + keep], current[:, :, :keep])
    return current


def build_profile(pulse_rows, firsts, phases, kernels, row_count):
    taps = kernels.shape[1]
    span = row_count + taps - 1
    window = shifted_window(pulse_rows, firsts, span)
    onehot = (phases[:, None] == jnp.arange(kernels.shape[0], dtype=jnp.int32)[None, :]).astype(
        jnp.float32
    )
    weights = jnp.dot(onehot, kernels, precision=lax.Precision.HIGHEST)
    summed_taps = jnp.zeros((pulse_rows.shape[0], 2, row_count), jnp.float32)
    for tap_index in range(taps):
        summed_taps = summed_taps + weights[:, tap_index, None, None] * window[
            :, :, tap_index : tap_index + row_count
        ].astype(jnp.float32)
    return summed_taps.astype(jnp.bfloat16)


def contract(left, right):
    return lax.dot_general(
        left, right, (((0,), (0,)), ((), ())), preferred_element_type=jnp.float32
    )


def project(profile, cosine, sine):
    real_part = contract(profile[:, 0], cosine) - contract(profile[:, 1], sine)
    imag_part = contract(profile[:, 0], sine) + contract(profile[:, 1], cosine)
    return jnp.stack([real_part, imag_part])


def per_device(echoes, offsets, phase_index, steering, kernels):
    pulse_dev = echoes.shape[0]
    tile_count = lax.axis_size("tile")
    group_count = lax.axis_size("pgroup")
    row_count = ROW_DEV * group_count
    columns = COL_DEV
    tile_index = lax.axis_index("tile")
    group_index = lax.axis_index("pgroup")
    delays = offsets[0]
    phase_rows = phase_index[0]
    rates = steering[0, 0]
    curves = steering[1, 0]
    normaliser = (STEPS * pulse_dev * group_count) ** (-0.5)
    local_starts = [(tile_index - distance) % tile_count * pulse_dev for distance in range(STEPS)]
    profiles = []
    blocks = [echoes]
    current = echoes
    for distance in range(1, STEPS):
        current = passed_along(current, "tile", 1)
        blocks.append(current)
    for distance in range(STEPS):
        first = local_starts[distance]
        firsts = lax.dynamic_slice_in_dim(delays, first, pulse_dev)
        phases = lax.dynamic_slice_in_dim(phase_rows, first, pulse_dev)
        profiles.append(build_profile(blocks[distance], firsts, phases, kernels, row_count))
    partial_value = jnp.zeros((2, row_count, columns), jnp.float32)
    for distance in range(STEPS):
        global_first = group_index * tile_count * pulse_dev + local_starts[distance]
        cosine, sine = steer_table(
            lax.dynamic_slice_in_dim(rates, global_first, pulse_dev),
            lax.dynamic_slice_in_dim(curves, global_first, pulse_dev),
            columns,
        )
        partial_value = partial_value + project(profiles[distance], cosine, sine)
    summed = lax.psum_scatter(partial_value, "pgroup", scatter_dimension=1, tiled=True)
    return summed * normaliser


def solution(mesh):
    placed = (
        P(("pgroup", "tile"), None, None),
        P("tile", "pgroup"),
        P("tile", "pgroup"),
        P(None, "tile", None),
        P(),
    )
    return jax.shard_map(
        per_device, mesh=mesh, in_specs=placed, out_specs=P(None, "pgroup", "tile"), check_vma=False
    )
```

profile of v0, /device:TPU:8, one launch (start us, length us, event | category | flops | bytes accessed | tf_op | source)
XLA Modules:
  0.0 329.4 jit_solution(6190629878541451019)
XLA Ops:
  6.5 1.8 copy.6
  8.4 1.9 collective-permute-start
  10.5 0.8 fusion.190
  12.1 0.9 fusion.127
  13.0 0.8 fusion.128
  14.1 0.3 fusion.10
  15.0 0.2 slice_select_fusion.38
  15.3 0.2 slice_select_fusion.37
  15.5 0.2 slice_select_fusion.36
  16.4 8.1 %collective-permute-done = bf16[64,2,4096]{2,0,1:T(8,128)(2,1)S(1)} collective-permute-done((bf16[64,2,4096]{2,0,1:T(8,128)(2,1)S(1)}, bf16[64,2,4096]{2,0,1:T(8,128)(2,1)S(1)}, u32[]{:S(2)}, u32[]{:S(2)}) %collective-permute-start) | collective-permute-done | bytes 1048608 | tf_op jit(solution)/shard_map/ppermute | solution.py:13
  24.5 0.3 fusion.11
  25.9 0.2 slice_select_fusion.29
  26.2 0.2 slice_select_fusion.28
  26.4 0.2 slice_select_fusion.27
  26.7 0.4 slice_select_fusion.26
  27.1 1.6 add_convert_fusion.3
  28.7 0.7 fusion.14
  29.4 0.7 fusion.15
  30.1 0.7 fusion.8
  30.8 1.6 add_convert_fusion.2
  32.4 2.1 collective-permute-start.1
  34.5 0.7 fusion.9
  35.2 0.7 fusion.16
  35.9 0.7 fusion.6
  36.6 0.7 fusion.17
  37.3 0.7 fusion.7
  38.1 10.4 %collective-permute-done.1 = bf16[64,2,4096]{2,0,1:T(8,128)(2,1)S(1)} collective-permute-done((bf16[64,2,4096]{2,0,1:T(8,128)(2,1)S(1)}, bf16[64,2,4096]{2,0,1:T(8,128)(2,1)S(1)}, u32[]{:S(2)}, u32[]{:S(2)}) %collective-permute-start.1) | collective-permute-done | bytes 1048608 | tf_op jit(solution)/shard_map/ppermute | solution.py:13
  48.5 0.3 fusion.12
  49.4 0.2 slice_select_fusion.24
  50.2 1.9 collective-permute-start.2
  52.6 14.5 %collective-permute-done.2 = bf16[64,2,4096]{2,0,1:T(8,128)(2,1)S(1)} collective-permute-done((bf16[64,2,4096]{2,0,1:T(8,128)(2,1)S(1)}, bf16[64,2,4096]{2,0,1:T(8,128)(2,1)S(1)}, u32[]{:S(2)}, u32[]{:S(2)}) %collective-permute-start.2) | collective-permute-done | bytes 1048608 | tf_op jit(solution)/shard_map/ppermute | solution.py:13
  67.1 0.3 fusion.13
  68.1 0.2 slice_select_fusion.17
  69.0 0.2 slice_select_fusion.13
  69.3 0.4 slice_select_fusion.12
  69.7 1.6 add_convert_fusion.1
  71.3 0.7 fusion.18
  72.0 0.7 fusion.19
  72.7 1.6 add_convert_fusion
  74.3 0.7 fusion.20
  75.0 0.7 fusion.21
  75.7 0.7 fusion.4
  76.4 0.7 fusion.5
  77.1 0.7 fusion.2
  77.8 0.7 fusion.3
  78.6 2.5 fusion.1
  81.1 239.6 %reduce-scatter.2.cloned.1.call-done = f32[2,256,256]{2,1,0:T(8,128)} async-done(((f32[2,2048,256]{2,1,0:T(8,128)}), f32[2,256,256]{2,1,0:T(8,128)}) %reduce-scatter.2.cloned.1.call-update) | async-done | bytes 524304 | tf_op jit(solution)/shard_map/reduce_scatter | solution.py:99
  320.7 1.9 broadcast_multiply_fusion
  (50 shorter events, 6.4 us)
Async XLA Ops:
  6.5 4.7 %copy-start = (f32[16,8]{0,1:T(8,128)S(1)}, f32[16,8]{0,1:T(8,128)}, u32[]{:S(2)}) copy-start(f32[16,8]{0,1:T(8,128)} %param.9) | copy-start | bytes 1540
  6.5 7.5 %copy-start.2 = (f32[2,1,32768]{2,1,0:T(1,128)S(1)}, f32[2,1,32768]{2,1,0:T(1,128)}, u32[]{:S(2)}) copy-start(f32[2,1,32768]{2,1,0:T(1,128)} %param.8) | copy-start | bytes 786436
  6.5 314.2 %reduce-scatter.2.cloned.1.call-start = ((), (), s32[]{:S(2)}) async-start(), calls=%async_computation.1 | async-start | bytes 4718592 | tf_op jit(solution)/shard_map/reduce_scatter | solution.py:99
  8.4 16.1 %collective-permute-start = (bf16[64,2,4096]{2,0,1:T(8,128)(2,1)S(1)}, bf16[64,2,4096]{2,0,1:T(8,128)(2,1)S(1)}, u32[]{:S(2)}, u32[]{:S(2)}) collective-permute-start(bf16[64,2,4096]{2,0,1:T(8,128)(2,1)S(1)} %copy.6), channel_id=1, source_target_pairs={{0,8},{8,16},{16,24},{24,32},{32,40},{40,48},{48,56},{56,64},{64,7... | collective-permute-start | bytes 3145736 | tf_op jit(solution)/shard_map/ppermute | solution.py:13
  32.4 16.1 %collective-permute-start.1 = (bf16[64,2,4096]{2,0,1:T(8,128)(2,1)S(1)}, bf16[64,2,4096]{2,0,1:T(8,128)(2,1)S(1)}, u32[]{:S(2)}, u32[]{:S(2)}) collective-permute-start(bf16[64,2,4096]{2,0,1:T(8,128)(2,1)S(1)} %collective-permute-done), channel_id=1, source_target_pairs={{0,8},{8,16},{16,24},{24,32},{32,40},{40,48},{48,56},{56,64},{64,7... | collective-permute-start | bytes 3145736 | tf_op jit(solution)/shard_map/ppermute | solution.py:13
  50.2 17.0 %collective-permute-start.2 = (bf16[64,2,4096]{2,0,1:T(8,128)(2,1)S(1)}, bf16[64,2,4096]{2,0,1:T(8,128)(2,1)S(1)}, u32[]{:S(2)}, u32[]{:S(2)}) collective-permute-start(bf16[64,2,4096]{2,0,1:T(8,128)(2,1)S(1)} %collective-permute-done.1), channel_id=1, source_target_pairs={{0,8},{8,16},{16,24},{24,32},{32,40},{40,48},{48,56},{56,64},{64,7... | collective-permute-start | bytes 3145736 | tf_op jit(solution)/shard_map/ppermute | solution.py:13
  81.1 241.5 %copy-start.1 = (f32[16,8]{0,1:T(8,128)S(1)}, f32[16,8]{0,1:T(8,128)}, u32[]{:S(2)}) copy-start(f32[16,8]{0,1:T(8,128)} %param.9) | copy-start | bytes 1540
Sparse Core Ops, SparseCore 0:
  81.2 239.4 reduce-scatter.1
where the time goes:
time: 330 us; the launch traced here: 329 us
  waiting for transfers between devices  273 us (83%)
  other arithmetic  21.8 us (7%)
  between operations  14 us (4%)
  matrix products  12.1 us (4%)
  starting transfers between devices  5.94 us (2%)
    reduce_scatter x1, waiting for transfers between devices, per_device(): lax.psum_scatter(partial_value, 'pgroup', scatter_dimension=1, tiled=True)  240 us
    ppermute x3, waiting for transfers between devices, passed_along(): lax.ppermute(shard, axis, [(i, (i + by) % length) for i in range(length)])  33.1 us
    dot_general x16, matrix products, contract(): lax.dot_general(left, right, (((0,), (0,)), ((), ())), preferred_element_...  11.3 us
    select_n x42, other arithmetic, shifted_window(): jnp.where(chosen, current[:, :, step_len:step_len + keep], current[:, :,...  9.34 us
  transfers between devices with their start and end apart: 4, of which 4 were waited for; matrix products, arithmetic and copies ran while one was open for 3% of the time, Pallas kernels for 0%

commit v1 on v0

v1 whole, which is shorter than its diff:
```python
import functools

import jax
import jax.numpy as jnp
from jax import lax
from jax.experimental import pallas as pl
from jax.experimental.pallas import tpu as pltpu
from jax.sharding import PartitionSpec as P

MESH = pl.DeviceIdType.MESH
LANES = 128
STEPS = 4
TAPS = 8
TILES = 64
XS = 4
PULSES = 64
COLS = 256
WIDE = 2 * PULSES
SLOTS = STEPS * XS
PIECES = 4
ROW_BLOCKS = 16
BLOCKS_IN = 32


def profile_kernel(echo_ref, table_ref, out_ref):
    lane = lax.broadcasted_iota(jnp.int32, (16, LANES), 1)

    def step(i, carry):
        d = i // 8
        q = i // 4 % 2
        part = i % 4
        row = pl.multiple_of(q * PULSES + part * 16, 16)
        trow = pl.multiple_of(d * PULSES + part * 16, 16)
        table = table_ref[pl.ds(trow, 16), :]
        first = jnp.broadcast_to(table[:, 0:1], (16, LANES)).astype(jnp.int32)
        weights = [jnp.broadcast_to(table[:, 1 + j : 2 + j], (16, LANES)) for j in range(TAPS)]
        fine = first % LANES
        index = (lane + fine) % LANES
        inside = lane + fine < LANES
        coarse = first // LANES
        bits = [(coarse >> level) % 2 == 1 for level in range(4)]
        memo = {}

        def once(f):
            def g(*key):
                k = (f.__name__,) + key
                if k not in memo:
                    memo[k] = f(*key)
                return memo[k]

            return g

        @once
        def loaded(s):
            s = min(s, BLOCKS_IN - 1)
            return echo_ref[pl.ds(row, 16), s * LANES : (s + 1) * LANES].astype(jnp.float32)

        @once
        def chosen(level, s):
            if level == 4:
                return loaded(s)
            return jnp.where(bits[level], chosen(level + 1, s + (1 << level)), chosen(level + 1, s))

        @once
        def turned(s):
            return jnp.take_along_axis(chosen(0, s), index, axis=1)

        @once
        def window(s):
            return jnp.where(inside, turned(s), turned(s + 1))

        @once
        def rolled(name, s, by):
            return pltpu.roll(makers[name](s), LANES - by, 1)

        def moved(name, s, by):
            if s == ROW_BLOCKS:
                return rolled(name, s, by)
            return jnp.where(lane < LANES - by, rolled(name, s, by), rolled(name, s + 1, by))

        @once
        def next_one(s):
            return moved("w", s, 1)

        @once
        def pair(m, s):
            return weights[2 * m] * window(s) + weights[2 * m + 1] * next_one(s)

        @once
        def quad(m, s):
            return pair(2 * m, s) + moved("p%d" % (2 * m + 1), s, 2)

        makers = {
            "w": window,
            "p1": functools.partial(pair, 1),
            "p3": functools.partial(pair, 3),
            "q1": functools.partial(quad, 1),
        }
        for s in range(ROW_BLOCKS):
            value = quad(0, s) + moved("q1", s, 4)
            out_ref[d * ROW_BLOCKS + s, pl.ds(row, 16), :] = value.astype(jnp.bfloat16)
        return carry

    lax.fori_loop(0, 8 * STEPS, step, 0)


def tables(rates, curves):
    v = lax.broadcasted_iota(jnp.int32, (COLS, LANES), 0).astype(jnp.float32) - (COLS - 1) / 2.0
    angle = rates * v + curves * (v * v / COLS)
    turn = jnp.floor(angle * 0.6366197723675814 + 0.5)
    r = angle - turn * 1.5703125
    r = r - turn * 4.837512969970703125e-4
    r = r - turn * 7.54978995489188216e-8
    z = r * r
    s = ((-1.9515295891e-4 * z + 8.3321608736e-3) * z - 1.6666654611e-1) * z * r + r
    c = ((2.443315711809948e-5 * z - 1.388731625493765e-3) * z + 4.166664568298827e-2) * z * z - 0.5 * z + 1.0
    half = lax.broadcasted_iota(jnp.int32, (COLS, LANES), 1) // PULSES
    quarter = turn.astype(jnp.int32) + half
    odd = (quarter & 1) == 1
    first = jnp.where(odd, s, c)
    second = jnp.where(odd, c, s)
    first = jnp.where(((quarter + 1) & 2) == 2, -first, first)
    second = jnp.where((quarter & 2) == 2, -second, second)
    return first.astype(jnp.bfloat16), second.astype(jnp.bfloat16)


def exchange_kernel(scale, prof_ref, steer_ref, out_ref, held, left, zsend, zheld, own, ssem, rsem, zssem, zrsem):
    t = lax.axis_index("tile")
    g = lax.axis_index("pgroup")
    x = g // 2
    zh = g % 2
    here = zh * TILES + t

    def place(n, sign):
        d = n // XS
        rel = n % XS
        other = (here + sign * d + 2 * TILES) % (2 * TILES)
        return other % TILES, (x + sign * rel + XS) % XS * 2 + other // TILES, other // TILES

    barrier = pltpu.get_barrier_semaphore()

    def greet(n, carry):
        pt, pg, _ = place(n, -1)
        pl.semaphore_signal(barrier, inc=1, device_id=(pt, pg), device_id_type=MESH)
        return carry

    lax.fori_loop(1, SLOTS, greet, 0)
    pl.semaphore_signal(barrier, inc=1, device_id=(t, x * 2 + 1 - zh), device_id_type=MESH)

    def steer(n, carry):
        d = n // XS
        rel = n % XS
        source = (here - d + 2 * TILES) % (2 * TILES)
        sg = (x + XS - rel) % XS * 2 + source // TILES
        line = sg * TILES + source % TILES
        re, im = tables(steer_ref[pl.ds(line, 1), :], steer_ref[pl.ds(8 * TILES + line, 1), :])
        at = pl.ds(pl.multiple_of(n * WIDE, WIDE), WIDE)
        left[0:COLS, at] = re
        left[COLS : 2 * COLS, at] = im
        return carry

    lax.fori_loop(0, SLOTS, steer, 0)
    pl.semaphore_wait(barrier, SLOTS)

    def chunk(j, px, ph):
        half = jnp.where(j < 2, 1 - ph, ph)
        return px * 4 + half * 2 + j % 2

    def send(j, n):
        pt, pg, ph = place(n, 1)
        d = n // XS
        return pltpu.make_async_remote_copy(
            src_ref=prof_ref.at[d * ROW_BLOCKS + chunk(j, pg // 2, ph)],
            dst_ref=held.at[j, pl.ds(pl.multiple_of(n * WIDE, WIDE), WIDE)],
            send_sem=ssem.at[j, n],
            recv_sem=rsem.at[j, n],
            device_id=(pt, pg),
            device_id_type=MESH,
        )

    def start_all(i, carry):
        send(i // (SLOTS - 1), i % (SLOTS - 1) + 1).start()
        return carry

    lax.fori_loop(0, PIECES * (SLOTS - 1), start_all, 0)

    def take(j, carry):
        held[j, 0:WIDE, :] = prof_ref[chunk(j, x, zh)]
        return carry

    lax.fori_loop(0, PIECES, take, 0)

    def arrived(j):
        def one(n, carry):
            send(j, n).wait_recv()
            return carry

        lax.fori_loop(1, SLOTS, one, 0)
        return jnp.dot(left[...], held[j], preferred_element_type=jnp.float32)

    def across(j):
        return pltpu.make_async_remote_copy(
            src_ref=zsend.at[j],
            dst_ref=zheld.at[j],
            send_sem=zssem.at[j],
            recv_sem=zrsem.at[j],
            device_id=(t, x * 2 + 1 - zh),
            device_id_type=MESH,
        )

    def far(j, carry):
        zsend[j] = arrived(j).astype(jnp.bfloat16)
        across(j).start()
        return carry

    def near(j, carry):
        own[j] = arrived(j + 2)
        return carry

    def finish(j, carry):
        across(j).wait_recv()
        total = (own[j] + zheld[j].astype(jnp.float32)) * scale
        rows = pl.ds(pl.multiple_of(j * LANES, LANES), LANES)
        out_ref[0, rows, :] = total[0:COLS].T
        out_ref[1, rows, :] = total[COLS : 2 * COLS].T
        return carry

    def drain(i, carry):
        send(i // (SLOTS - 1), i % (SLOTS - 1) + 1).wait_send()
        return carry

    lax.fori_loop(0, 2, far, 0)
    lax.fori_loop(0, 2, near, 0)
    lax.fori_loop(0, 2, finish, 0)
    lax.fori_loop(0, PIECES * (SLOTS - 1), drain, 0)
    across(0).wait_send()
    across(1).wait_send()


def per_device(echoes, offsets, phase_index, steering, kernels):
    t = lax.axis_index("tile")
    scale = (STEPS * PULSES * lax.axis_size("pgroup")) ** (-0.5)
    vmem = pl.BlockSpec(memory_space=pltpu.VMEM)

    def near(a):
        blocks = a.reshape(TILES, PULSES)
        return lax.dynamic_slice_in_dim(jnp.concatenate([blocks[TILES - 3 :], blocks]), t, STEPS)[::-1]

    firsts = near(offsets).astype(jnp.float32)
    phases = near(phase_index)
    onehot = (phases[:, :, None] == jnp.arange(kernels.shape[0], dtype=jnp.int32)).astype(jnp.float32)
    weights = jnp.dot(onehot, kernels, precision=lax.Precision.HIGHEST)
    table = jnp.concatenate([firsts[:, :, None], weights], 2)
    table = jnp.pad(table, ((0, 0), (0, 0), (0, LANES - 1 - TAPS)))
    sent = [table[0]]
    for d in range(1, STEPS):
        sent.append(lax.ppermute(table[d], "tile", [(i, (i - d) % TILES) for i in range(TILES)]))
    table = jnp.concatenate(sent)
    rows = jnp.transpose(echoes, (1, 0, 2)).reshape(WIDE, echoes.shape[2])
    profile = pl.pallas_call(
        profile_kernel,
        out_shape=jax.ShapeDtypeStruct((STEPS * ROW_BLOCKS, WIDE, LANES), jnp.bfloat16),
        in_specs=[vmem, vmem],
        out_specs=vmem,
    )(rows, table)
    steer = steering.reshape(-1, PULSES)
    steer = jnp.concatenate([steer, steer], 1)
    return pl.pallas_call(
        functools.partial(exchange_kernel, scale),
        out_shape=jax.ShapeDtypeStruct((2, COLS, COLS), jnp.float32),
        in_specs=[vmem, vmem],
        out_specs=vmem,
        scratch_shapes=[
            pltpu.VMEM((PIECES, SLOTS * WIDE, LANES), jnp.bfloat16),
            pltpu.VMEM((2 * COLS, SLOTS * WIDE), jnp.bfloat16),
            pltpu.VMEM((2, 2 * COLS, LANES), jnp.bfloat16),
            pltpu.VMEM((2, 2 * COLS, LANES), jnp.bfloat16),
            pltpu.VMEM((2, 2 * COLS, LANES), jnp.float32),
            pltpu.SemaphoreType.DMA((PIECES, SLOTS)),
            pltpu.SemaphoreType.DMA((PIECES, SLOTS)),
            pltpu.SemaphoreType.DMA((2,)),
            pltpu.SemaphoreType.DMA((2,)),
        ],
        compiler_params=pltpu.CompilerParams(collective_id=0, has_side_effects=True),
    )(profile, steer)


def solution(mesh):
    placed = (
        P(("pgroup", "tile"), None, None),
        P("tile", "pgroup"),
        P("tile", "pgroup"),
        P(None, "tile", None),
        P(),
    )
    return jax.shard_map(
        per_device, mesh=mesh, in_specs=placed, out_specs=P(None, "pgroup", "tile"), check_vma=False
    )
```

time: 330 us -> 120 us (0.36)
  waiting for transfers between devices: 273 us -> 0.01 us
  Pallas kernels: 0 us -> 88.2 us
  other arithmetic: 21.8 us -> 6.32 us
  between operations: 14 us -> 0.1 us
  starting transfers between devices: 5.94 us -> 19.3 us
  matrix products: 12.1 us -> 0.26 us
    reduce_scatter x1 -> x0, waiting for transfers between devices: 240 us -> none  [per_device(): lax.psum_scatter(partial_value, 'pgroup', scatter_dimension=1, tiled=True)]
    pallas_call x0 -> x2, Pallas kernels: none -> 88.2 us  [the longest x1 70.4 us: per_device(): pl.pallas_call(functools.partial(exchange_kernel, scale), out_shape=jax.S...]
    ppermute x3, waiting for transfers between devices: 33.1 us -> 0.01 us  [per_device(): lax.ppermute(table[d], 'tile', [(i, (i - d) % TILES) for i in range(TILES)])]
    ppermute x3, starting transfers between devices: 5.94 us -> 19.3 us  [per_device(): lax.ppermute(table[d], 'tile', [(i, (i - d) % TILES) for i in range(TILES)])]
    dot_general x20 -> x1, matrix products: 12.1 us -> 0.26 us  [per_device(): weights = jnp.dot(onehot, kernels, precision=lax.Precision.HIGHEST)]
    select_n x42 -> x0, other arithmetic: 9.34 us -> none  [shifted_window(): jnp.where(chosen, current[:, :, step_len:step_len + keep], current[:, :,...]
    convert_element_type x4 -> x0, other arithmetic: 6.22 us -> none  [build_profile(): return summed_taps.astype(jnp.bfloat16)]
    unnamed x0 -> x3, other arithmetic: none -> 4.52 us
  transfers between devices with their start and end apart: 4 -> 3, of which waited for: 4 -> 0; matrix products, arithmetic and copies ran while one was open for 3% -> 4% of each run, Pallas kernels for 0% -> 0%
where the time goes in v1:
time: 120 us
  Pallas kernels  88.2 us (74%)
  starting transfers between devices  19.3 us (16%)
  other arithmetic  6.32 us (5%)
  local copies, waits for them, and re-layouts  5.57 us (5%)
    pallas_call x1, Pallas kernels, per_device(): pl.pallas_call(functools.partial(exchange_kernel, scale), out_shape=jax.S...  70.4 us
    ppermute x3, starting transfers between devices, per_device(): lax.ppermute(table[d], 'tile', [(i, (i - d) % TILES) for i in range(TILES)])  19.3 us
    pallas_call x1, Pallas kernels, per_device(): pl.pallas_call(profile_kernel, out_shape=jax.ShapeDtypeStruct((STEPS * RO...  17.8 us
    unnamed x3, other arithmetic  4.52 us
  transfers between devices with their start and end apart: 3, of which 0 were waited for; matrix products, arithmetic and copies ran while one was open for 4% of the time, Pallas kernels for 0%

profile of v1, /device:TPU:8, one launch (start us, length us, event | category | flops | bytes accessed | tf_op | source)
XLA Modules:
  0.0 119.8 jit_solution(4908677142772292949)
XLA Ops:
  0.0 0.0 copy-start
  0.0 0.0 copy-start.1
  0.0 0.5 broadcast.22
  0.5 1.4 %reduce.16 = s32[4096]{0:T(1024)S(1)} reduce(s32[1,4096]{1,0:T(1,128)} %param.6, s32[]{:T(128)} %broadcast.22), dimensions={0}, to_apply=%param.6.reduce_sub_computation.3 | reduce | bytes 32772 | tf_op args[1]
  1.9 0.8 slice_reduce_fusion
  2.7 1.4 %reduce.15 = s32[4096]{0:T(1024)S(1)} reduce(s32[1,4096]{1,0:T(1,128)} %param.7, s32[]{:T(128)} %broadcast.22), dimensions={0}, to_apply=%param.7.reduce_sub_computation.3 | reduce | bytes 32772 | tf_op args[2]
  4.1 0.1 reshape.16
  4.2 0.1 slice.25
  4.3 0.1 copy.15
  4.5 0.1 reshape.17
  4.5 0.1 slice.27
  4.7 0.0 copy-done
  4.7 0.3 fusion.1
  4.9 0.1 select_maximum_fusion
  5.1 1.9 %collective-permute-start = (f32[64,128]{1,0:T(8,128)S(1)}, f32[64,128]{1,0:T(8,128)S(1)}, u32[]{:S(2)}, u32[]{:S(2)}) collective-permute-start(f32[64,128]{1,0:T(8,128)S(1)} %get-tuple-element.7), channel_id=1, source_target_pairs={{0,504},{8,0},{16,8},{24,16},{32,24},{40,32},{48,40},{56,48},{64,5... | collective-permute-start | bytes 98312 | tf_op jit(solution)/shard_map/ppermute | solution.py:257
  7.0 15.5 %collective-permute-start.1 = (f32[64,128]{1,0:T(8,128)S(1)}, f32[64,128]{1,0:T(8,128)S(1)}, u32[]{:S(2)}, u32[]{:S(2)}) collective-permute-start(f32[64,128]{1,0:T(8,128)S(1)} %get-tuple-element.6), channel_id=1, source_target_pairs={{0,496},{8,504},{16,0},{24,8},{32,16},{40,24},{48,32},{56,40},{64,... | collective-permute-start | bytes 98312 | tf_op jit(solution)/shard_map/ppermute | solution.py:257
  22.5 1.9 %collective-permute-start.2 = (f32[64,128]{1,0:T(8,128)S(1)}, f32[64,128]{1,0:T(8,128)S(1)}, u32[]{:S(2)}, u32[]{:S(2)}) collective-permute-start(f32[64,128]{1,0:T(8,128)S(1)} %get-tuple-element.8), channel_id=1, source_target_pairs={{0,488},{8,496},{16,504},{24,0},{32,8},{40,16},{48,24},{56,32},{64... | collective-permute-start | bytes 98312 | tf_op jit(solution)/shard_map/ppermute | solution.py:257
  24.4 1.7 %reduce.4 = f32[2,32768]{1,0:T(2,128)S(1)} reduce(f32[2,1,32768]{2,1,0:T(1,128)} %param.8, f32[]{:T(128)} %constant.22), dimensions={1}, to_apply=%param.8.reduce_sub_computation | reduce | bytes 524292 | tf_op args[3]
  26.1 0.3 reshape.18
  26.5 1.0 pad_maximum_fusion.steer_ref
  27.5 0.0 copy-done.1
  27.5 1.6 %copy.14 = bf16[2,64,4096]{2,1,0:T(8,128)(2,1)} copy(bf16[2,64,4096]{2,0,1:T(2,128)(2,1)S(1)} %bitcast.16) | data formatting | bytes 2097152 | tf_op jit(solution)/shard_map/transpose | solution.py:259
  29.0 0.0 collective-permute-done
  29.0 0.0 collective-permute-done.1
  29.0 0.0 collective-permute-done.2
  29.1 0.7 pad_maximum_fusion.1.table_ref
  29.7 17.8 %shard_map.55.prof_ref = bf16[64,128,128]{2,1,0:T(8,128)(2,1)} custom-call(bf16[128,4096]{1,0:T(8,128)(2,1)} %bitcast.15, f32[256,128]{1,0:T(8,128)} %pad_maximum_fusion.1.table_ref), custom_call_target="tpu_custom_call" | custom-call | tf_op jit(solution)/shard_map/pallas_call | solution.py:260
  47.5 70.4 %shard_map.56 = f32[2,256,256]{2,1,0:T(8,128)} custom-call(bf16[64,128,128]{2,1,0:T(8,128)(2,1)} %shard_map.55.prof_ref, f32[1024,128]{1,0:T(8,128)} %pad_maximum_fusion.steer_ref), custom_call_target="tpu_custom_call" | custom-call | tf_op jit(solution)/shard_map/pallas_call | solution.py:268
  117.9 1.9 %copy.19 = f32[2,256,256]{2,1,0:T(8,128)} copy(f32[2,256,256]{2,1,0:T(8,128)} %shard_map.56) | data formatting | bytes 1048576
  (6 shorter events, 0.1 us)
Async XLA Ops:
  0.0 4.7 %copy-start = (f32[16,8]{0,1:T(8,128)S(1)}, f32[16,8]{0,1:T(8,128)}, u32[]{:S(2)}) copy-start(f32[16,8]{0,1:T(8,128)} %param.9) | copy-start | bytes 1540
  0.0 27.5 %copy-start.1 = (bf16[64,2,4096]{2,1,0:T(2,128)(2,1)S(1)}, bf16[64,2,4096]{2,1,0:T(2,128)(2,1)}, u32[]{:S(2)}) copy-start(bf16[64,2,4096]{2,1,0:T(2,128)(2,1)} %param.5) | copy-start | bytes 3145732
  5.1 24.0 %collective-permute-start = (f32[64,128]{1,0:T(8,128)S(1)}, f32[64,128]{1,0:T(8,128)S(1)}, u32[]{:S(2)}, u32[]{:S(2)}) collective-permute-start(f32[64,128]{1,0:T(8,128)S(1)} %get-tuple-element.7), channel_id=1, source_target_pairs={{0,504},{8,0},{16,8},{24,16},{32,24},{40,32},{48,40},{56,48},{64,5... | collective-permute-start | bytes 98312 | tf_op jit(solution)/shard_map/ppermute | solution.py:257
  7.0 22.1 %collective-permute-start.1 = (f32[64,128]{1,0:T(8,128)S(1)}, f32[64,128]{1,0:T(8,128)S(1)}, u32[]{:S(2)}, u32[]{:S(2)}) collective-permute-start(f32[64,128]{1,0:T(8,128)S(1)} %get-tuple-element.6), channel_id=1, source_target_pairs={{0,496},{8,504},{16,0},{24,8},{32,16},{40,24},{48,32},{56,40},{64,... | collective-permute-start | bytes 98312 | tf_op jit(solution)/shard_map/ppermute | solution.py:257
  22.5 6.6 %collective-permute-start.2 = (f32[64,128]{1,0:T(8,128)S(1)}, f32[64,128]{1,0:T(8,128)S(1)}, u32[]{:S(2)}, u32[]{:S(2)}) collective-permute-start(f32[64,128]{1,0:T(8,128)S(1)} %get-tuple-element.8), channel_id=1, source_target_pairs={{0,488},{8,496},{16,504},{24,0},{32,8},{40,16},{48,24},{56,32},{64... | collective-permute-start | bytes 98312 | tf_op jit(solution)/shard_map/ppermute | solution.py:257

commit v2 on v1

v2 whole, which is shorter than its diff:
```python
import functools

import jax
import jax.numpy as jnp
from jax import lax
from jax.experimental import pallas as pl
from jax.experimental.pallas import tpu as pltpu
from jax.sharding import PartitionSpec as P

MESH = pl.DeviceIdType.MESH
LANES = 128
STEPS = 4
TAPS = 8
TILES = 64
XS = 4
PULSES = 64
COLS = 256
WIDE = 2 * PULSES
SLOTS = STEPS * XS
PIECES = 4
ROW_BLOCKS = 16
BLOCKS_IN = 32
SIN = (6.2831853, -41.3417004, 81.6051314, -76.7030154, 42.025927, -14.8998467, 3.23813751)
COS = (1, -19.7392087, 64.9393891, -85.4566583, 60.2421313, -26.4046682, 7.80013142, -1.45311229)


def build_profile(echo_ref, table_ref, out_ref, d, part):
    lane = lax.broadcasted_iota(jnp.int32, (16, LANES), 1)
    trow = pl.multiple_of(d * PULSES + part * 16, 16)
    table = table_ref[pl.ds(trow, 16), :]
    first = jnp.broadcast_to(table[:, TAPS : TAPS + 1], (16, LANES)).astype(jnp.int32)
    weights = [jnp.broadcast_to(table[:, j : 1 + j], (16, LANES)) for j in range(TAPS)]
    fine = first & (LANES - 1)
    ahead = lane + fine
    index = ahead & (LANES - 1)
    inside = ahead < LANES
    bits = []
    for level in range(4):
        on = (first >> (7 + level)) & 1
        bits.append(on.astype(jnp.float32).astype(jnp.bfloat16) > 0.5)
    for q in range(2):
        row = pl.multiple_of(q * PULSES + part * 16, 16)
        memo = {}

        def once(f, memo=memo):
            def g(*key):
                k = (f.__name__,) + key
                if k not in memo:
                    memo[k] = f(*key)
                return memo[k]

            return g

        @once
        def loaded(s, row=row):
            s = min(s, BLOCKS_IN - 1)
            return echo_ref[pl.ds(row, 16), s * LANES : (s + 1) * LANES]

        @once
        def chosen(level, s):
            if level == 4:
                return loaded(s)
            return jnp.where(bits[level], chosen(level + 1, s + (1 << level)), chosen(level + 1, s))

        @once
        def turned(s):
            return jnp.take_along_axis(chosen(0, s).astype(jnp.float32), index, axis=1)

        @once
        def window(s):
            return jnp.where(inside, turned(s), turned(s + 1))

        @once
        def rolled(name, s, by):
            return pltpu.roll(makers[name](s), LANES - by, 1)

        def moved(name, s, by):
            if s == ROW_BLOCKS:
                return rolled(name, s, by)
            return jnp.where(lane < LANES - by, rolled(name, s, by), rolled(name, s + 1, by))

        @once
        def next_one(s):
            return moved("w", s, 1)

        @once
        def pair(m, s):
            return weights[2 * m] * window(s) + weights[2 * m + 1] * next_one(s)

        @once
        def quad(m, s):
            return pair(2 * m, s) + moved("p%d" % (2 * m + 1), s, 2)

        makers = {
            "w": window,
            "p1": functools.partial(pair, 1),
            "p3": functools.partial(pair, 3),
            "q1": functools.partial(quad, 1),
        }
        for s in range(ROW_BLOCKS):
            value = quad(0, s) + moved("q1", s, 4)
            out_ref[d * ROW_BLOCKS + s, pl.ds(row, 16), :] = value.astype(jnp.bfloat16)


def half_row(ref, block, *lead):
    at = pl.ds(pl.multiple_of(block // 2 * LANES, LANES), LANES)
    row = ref[(*lead, slice(None), at)] if lead else ref[:, at]
    return jnp.where(block % 2 == 1, pltpu.roll(row, PULSES, 1), row)


def tables(rates, curves, phase):
    v = lax.broadcasted_iota(jnp.int32, (COLS, LANES), 0).astype(jnp.float32) - (COLS - 1) / 2.0
    turns = rates * v + curves * (v * v * (1.0 / COLS)) + phase
    whole = (turns + 12582912.0) - 12582912.0
    f = turns - whole
    z = f * f
    s = SIN[-1]
    for k in SIN[-2::-1]:
        s = s * z + k
    s = s * f
    c = COS[-1]
    for k in COS[-2::-1]:
        c = c * z + k
    return c.astype(jnp.bfloat16), s.astype(jnp.bfloat16)


def strip_kernel(
    scale, echo_ref, offs_ref, phase_ref, steer_ref, kern_ref, out_ref,
    prof, tab, tsend, kpad, held, left, zsend, zheld, own, tssem, trsem, ssem, rsem, zssem, zrsem,
):
    t = lax.axis_index("tile")
    g = lax.axis_index("pgroup")
    x = g // 2
    zh = g % 2
    here = zh * TILES + t

    def place(n, sign):
        d = n // XS
        rel = n % XS
        other = (here + sign * d + 2 * TILES) % (2 * TILES)
        return other % TILES, (x + sign * rel + XS) % XS * 2 + other // TILES, other // TILES

    barrier = pltpu.get_barrier_semaphore()

    def greet(n, carry):
        pt, pg, _ = place(n, -1)
        pl.semaphore_signal(barrier, inc=1, device_id=(pt, pg), device_id_type=MESH)
        return carry

    lax.fori_loop(1, SLOTS, greet, 0)
    pl.semaphore_signal(barrier, inc=1, device_id=(t, x * 2 + 1 - zh), device_id_type=MESH)
    for d in range(1, STEPS):
        pl.semaphore_signal(barrier, inc=1, device_id=((t + d) % TILES, g), device_id_type=MESH)

    kpad[...] = jnp.zeros_like(kpad)
    kpad[0 : kern_ref.shape[0], 0:TAPS] = kern_ref[...]
    lane = lax.broadcasted_iota(jnp.int32, (PULSES, LANES), 1)
    eye = lane == lax.broadcasted_iota(jnp.int32, (PULSES, LANES), 0)

    def window_table(d):
        block = (t + TILES - d) % TILES
        firsts = half_row(offs_ref, block).astype(jnp.float32)
        phases = half_row(phase_ref, block).astype(jnp.float32)
        first = jnp.sum(jnp.where(eye, firsts, 0.0), axis=1, keepdims=True)
        kind = jnp.sum(jnp.where(eye, phases, 0.0), axis=1, keepdims=True)
        onehot = jnp.where(lane.astype(jnp.float32) == kind, 1.0, 0.0)
        weights = jnp.dot(
            onehot, kpad[...], precision=lax.Precision.HIGHEST, preferred_element_type=jnp.float32
        )
        return jnp.where(lane == TAPS, first, weights)

    tab[0:PULSES] = window_table(0)
    for d in range(1, STEPS):
        tsend[d - 1] = window_table(d)

    def table_copy(d):
        return pltpu.make_async_remote_copy(
            src_ref=tsend.at[d - 1],
            dst_ref=tab.at[pl.ds(pl.multiple_of(d * PULSES, PULSES), PULSES)],
            send_sem=tssem.at[d],
            recv_sem=trsem.at[d],
            device_id=((t + TILES - d) % TILES, g),
            device_id_type=MESH,
        )

    lane_row = lax.broadcasted_iota(jnp.int32, (1, LANES), 1)
    quarter = jnp.where(lane_row < PULSES, 0.0, 0.25)

    def steer(n, carry):
        d = n // XS
        rel = n % XS
        source = (here - d + 2 * TILES) % (2 * TILES)
        sg = (x + XS - rel) % XS * 2 + source // TILES
        line = sg * TILES + source % TILES

        def both(i):
            row = half_row(steer_ref, line, i)
            return jnp.where(lane_row < PULSES, row, pltpu.roll(row, PULSES, 1)) * (0.5 / 3.141592653589793)

        re, im = tables(both(0), both(1), quarter)
        at = pl.ds(pl.multiple_of(n * WIDE, WIDE), WIDE)
        left[0:COLS, at] = re
        left[COLS : 2 * COLS, at] = im
        return carry

    lax.fori_loop(0, SLOTS, steer, 0)
    pl.semaphore_wait(barrier, SLOTS + STEPS - 1)
    for d in range(1, STEPS):
        table_copy(d).start()

    def chunk(j, px, ph):
        half = jnp.where(j < 2, 1 - ph, ph)
        return px * 4 + half * 2 + j % 2

    def send(j, n):
        pt, pg, ph = place(n, 1)
        d = n // XS
        return pltpu.make_async_remote_copy(
            src_ref=prof.at[d * ROW_BLOCKS + chunk(j, pg // 2, ph)],
            dst_ref=held.at[j, pl.ds(pl.multiple_of(n * WIDE, WIDE), WIDE)],
            send_sem=ssem.at[j, n],
            recv_sem=rsem.at[j, n],
            device_id=(pt, pg),
            device_id_type=MESH,
        )

    def distance(i, carry):
        d = (STEPS - i) % STEPS

        @pl.when(d > 0)
        def _():
            table_copy(d).wait_recv()

        def part(p, c):
            build_profile(echo_ref, tab, prof, d, p)
            return c

        lax.fori_loop(0, PULSES // 16, part, 0)

        def early(m, c):
            n = d * XS + m % XS

            @pl.when(n > 0)
            def _():
                send(m // XS, n).start()

            return c

        lax.fori_loop(0, 2 * XS, early, 0)
        return carry

    lax.fori_loop(0, STEPS, distance, 0)

    def late(i, carry):
        send(2 + i // (SLOTS - 1), i % (SLOTS - 1) + 1).start()
        return carry

    lax.fori_loop(0, 2 * (SLOTS - 1), late, 0)

    def take(j, carry):
        held[j, 0:WIDE, :] = prof[chunk(j, x, zh)]
        return carry

    lax.fori_loop(0, PIECES, take, 0)

    def arrived(j):
        def one(n, carry):
            send(j, n).wait_recv()
            return carry

        lax.fori_loop(1, SLOTS, one, 0)
        return jnp.dot(left[...], held[j], preferred_element_type=jnp.float32)

    def across(j):
        return pltpu.make_async_remote_copy(
            src_ref=zsend.at[j],
            dst_ref=zheld.at[j],
            send_sem=zssem.at[j],
            recv_sem=zrsem.at[j],
            device_id=(t, x * 2 + 1 - zh),
            device_id_type=MESH,
        )

    def far(j, carry):
        zsend[j] = arrived(j).astype(jnp.bfloat16)
        across(j).start()
        return carry

    def near(j, carry):
        own[j] = arrived(j + 2)
        return carry

    def finish(j, carry):
        across(j).wait_recv()
        total = (own[j] + zheld[j].astype(jnp.float32)) * scale
        rows = pl.ds(pl.multiple_of(j * LANES, LANES), LANES)
        out_ref[0, rows, :] = total[0:COLS].T
        out_ref[1, rows, :] = total[COLS : 2 * COLS].T
        return carry

    def drain(i, carry):
        send(i // (SLOTS - 1), i % (SLOTS - 1) + 1).wait_send()
        return carry

    lax.fori_loop(0, 2, far, 0)
    lax.fori_loop(0, 2, near, 0)
    lax.fori_loop(0, 2, finish, 0)
    lax.fori_loop(0, PIECES * (SLOTS - 1), drain, 0)
    for d in range(1, STEPS):
        table_copy(d).wait_send()
    across(0).wait_send()
    across(1).wait_send()


def per_device(echoes, offsets, phase_index, steering, kernels):
    scale = (STEPS * PULSES * lax.axis_size("pgroup")) ** (-0.5)
    vmem = pl.BlockSpec(memory_space=pltpu.VMEM)
    rows = jnp.transpose(echoes, (1, 0, 2)).reshape(WIDE, echoes.shape[2])
    dma = pltpu.SemaphoreType.DMA
    return pl.pallas_call(
        functools.partial(strip_kernel, scale),
        out_shape=jax.ShapeDtypeStruct((2, COLS, COLS), jnp.float32),
        in_specs=[vmem] * 5,
        out_specs=vmem,
        scratch_shapes=[
            pltpu.VMEM((STEPS * ROW_BLOCKS, WIDE, LANES), jnp.bfloat16),
            pltpu.VMEM((STEPS * PULSES, LANES), jnp.float32),
            pltpu.VMEM((STEPS - 1, PULSES, LANES), jnp.float32),
            pltpu.VMEM((LANES, LANES), jnp.float32),
            pltpu.VMEM((PIECES, SLOTS * WIDE, LANES), jnp.bfloat16),
            pltpu.VMEM((2 * COLS, SLOTS * WIDE), jnp.bfloat16),
            pltpu.VMEM((2, 2 * COLS, LANES), jnp.bfloat16),
            pltpu.VMEM((2, 2 * COLS, LANES), jnp.bfloat16),
            pltpu.VMEM((2, 2 * COLS, LANES), jnp.float32),
            dma((STEPS,)),
            dma((STEPS,)),
            dma((PIECES, SLOTS)),
            dma((PIECES, SLOTS)),
            dma((2,)),
            dma((2,)),
        ],
        compiler_params=pltpu.CompilerParams(collective_id=0, has_side_effects=True),
    )(rows, offsets, phase_index, steering, kernels)


def solution(mesh):
    placed = (
        P(("pgroup", "tile"), None, None),
        P("tile", "pgroup"),
        P("tile", "pgroup"),
        P(None, "tile", None),
        P(),
    )
    return jax.shard_map(
        per_device, mesh=mesh, in_specs=placed, out_specs=P(None, "pgroup", "tile"), check_vma=False
    )
```

time: 120 us -> 91.8 us (0.77)
  the two profiles are of different devices: /device:TPU:8 before, /device:TPU:10 now
where the time goes in v2:
time: 91.8 us; the launch traced here: 91.6 us
  Pallas kernels  85.6 us (93%)
  local copies, waits for them, and re-layouts  6.02 us (7%)
    pallas_call x1, Pallas kernels, per_device(): pl.pallas_call(functools.partial(strip_kernel, scale), out_shape=jax.Shap...  85.6 us
    unnamed x2, local copies, waits for them, and re-layouts  3.22 us
    transpose x1, local copies, waits for them, and re-layouts, per_device(): rows = jnp.transpose(echoes, (1, 0, 2)).reshape(WIDE, echoes.shape[2])  2.79 us

profile of v2, /device:TPU:10, one launch (start us, length us, event | category | flops | bytes accessed | tf_op | source)
XLA Modules:
  0.0 91.6 jit_solution(7952967770211787850)
XLA Ops:
  0.0 1.4 %copy.7.kern_ref = f32[16,8]{1,0:T(8,128)} copy(f32[16,8]{0,1:T(8,128)} %param.9) | data formatting | bytes 1024 | tf_op args[4]
  1.4 2.8 %copy.6 = bf16[2,64,4096]{2,1,0:T(8,128)(2,1)} copy(bf16[2,64,4096]{2,0,1:T(2,128)(2,1)} %bitcast.3) | data formatting | bytes 2097152 | tf_op jit(solution)/shard_map/transpose | solution.py:318
  4.2 85.6 %shard_map.55 = f32[2,256,256]{2,1,0:T(8,128)} custom-call(bf16[128,4096]{1,0:T(8,128)(2,1)} %bitcast.2, s32[1,4096]{1,0:T(1,128)} %offs_ref.1, s32[1,4096]{1,0:T(1,128)} %phase_ref.1, f32[2,1,32768]{2,1,0:T(1,128)} %steer_ref.1, f32[16,8]{1,0:T(8,128)} %copy.7.kern_ref), custom_call_target="tpu_custom_call" | custom-call | tf_op jit(solution)/shard_map/pallas_call | solution.py:320
  89.7 1.9 %copy.9 = f32[2,256,256]{2,1,0:T(8,128)} copy(f32[2,256,256]{2,1,0:T(8,128)} %shard_map.55) | data formatting | bytes 1048576

commit v3 on v2

--- a/solution.py
+++ b/solution.py
@@ -18,6 +18,9 @@
 WIDE = 2 * PULSES
 SLOTS = STEPS * XS
 PIECES = 4
+LEG = 32
+QUARTERS = 8
+QROWS = 64
 ROW_BLOCKS = 16
 BLOCKS_IN = 32
 SIN = (6.2831853, -41.3417004, 81.6051314, -76.7030154, 42.025927, -14.8998467, 3.23813751)
@@ -103,9 +106,9 @@
 
 
 def half_row(ref, block, *lead):
-    at = pl.ds(pl.multiple_of(block // 2 * LANES, LANES), LANES)
+    at = pl.ds(pl.multiple_of((block >> 1) * LANES, LANES), LANES)
     row = ref[(*lead, slice(None), at)] if lead else ref[:, at]
-    return jnp.where(block % 2 == 1, pltpu.roll(row, PULSES, 1), row)
+    return jnp.where((block & 1) == 1, pltpu.roll(row, PULSES, 1), row)
 
 
 def tables(rates, curves, phase):
@@ -126,19 +129,19 @@
 
 def strip_kernel(
     scale, echo_ref, offs_ref, phase_ref, steer_ref, kern_ref, out_ref,
-    prof, tab, tsend, kpad, held, left, zsend, zheld, own, tssem, trsem, ssem, rsem, zssem, zrsem,
+    prof, tab, tsend, kpad, held, left, zsend, relay, zheld, own, tssem, trsem, ssem, rsem, zssem, zrsem,
 ):
     t = lax.axis_index("tile")
     g = lax.axis_index("pgroup")
-    x = g // 2
-    zh = g % 2
+    x = g >> 1
+    zh = g & 1
     here = zh * TILES + t
 
     def place(n, sign):
-        d = n // XS
-        rel = n % XS
-        other = (here + sign * d + 2 * TILES) % (2 * TILES)
-        return other % TILES, (x + sign * rel + XS) % XS * 2 + other // TILES, other // TILES
+        d = n >> 2
+        rel = n & (XS - 1)
+        other = (here + sign * d) & (2 * TILES - 1)
+        return other & (TILES - 1), ((x + sign * rel) & (XS - 1)) * 2 + (other >> 6), other >> 6
 
     barrier = pltpu.get_barrier_semaphore()
 
@@ -148,24 +151,33 @@
         return carry
 
     lax.fori_loop(1, SLOTS, greet, 0)
-    pl.semaphore_signal(barrier, inc=1, device_id=(t, x * 2 + 1 - zh), device_id_type=MESH)
+    def along(by):
+        other = (here + by) & (2 * TILES - 1)
+        return other & (TILES - 1), x * 2 + (other >> 6)
+
+    for by in (-LEG, LEG):
+        pl.semaphore_signal(barrier, inc=1, device_id=along(by), device_id_type=MESH)
     for d in range(1, STEPS):
-        pl.semaphore_signal(barrier, inc=1, device_id=((t + d) % TILES, g), device_id_type=MESH)
+        pl.semaphore_signal(barrier, inc=1, device_id=((t + d) & (TILES - 1), g), device_id_type=MESH)
 
     kpad[...] = jnp.zeros_like(kpad)
-    kpad[0 : kern_ref.shape[0], 0:TAPS] = kern_ref[...]
+    kpad[0:TAPS, 0 : kern_ref.shape[1]] = kern_ref[...]
     lane = lax.broadcasted_iota(jnp.int32, (PULSES, LANES), 1)
     eye = lane == lax.broadcasted_iota(jnp.int32, (PULSES, LANES), 0)
 
     def window_table(d):
-        block = (t + TILES - d) % TILES
+        block = (t - d) & (TILES - 1)
         firsts = half_row(offs_ref, block).astype(jnp.float32)
         phases = half_row(phase_ref, block).astype(jnp.float32)
         first = jnp.sum(jnp.where(eye, firsts, 0.0), axis=1, keepdims=True)
         kind = jnp.sum(jnp.where(eye, phases, 0.0), axis=1, keepdims=True)
         onehot = jnp.where(lane.astype(jnp.float32) == kind, 1.0, 0.0)
-        weights = jnp.dot(
-            onehot, kpad[...], precision=lax.Precision.HIGHEST, preferred_element_type=jnp.float32
+        weights = lax.dot_general(
+            onehot,
+            kpad[...],
+            (((1,), (1,)), ((), ())),
+            precision=lax.Precision.HIGHEST,
+            preferred_element_type=jnp.float32,
         )
         return jnp.where(lane == TAPS, first, weights)
 
@@ -179,7 +191,7 @@
             dst_ref=tab.at[pl.ds(pl.multiple_of(d * PULSES, PULSES), PULSES)],
             send_sem=tssem.at[d],
             recv_sem=trsem.at[d],
-            device_id=((t + TILES - d) % TILES, g),
+            device_id=((t - d) & (TILES - 1), g),
             device_id_type=MESH,
         )
 
@@ -187,11 +199,10 @@
     quarter = jnp.where(lane_row < PULSES, 0.0, 0.25)
 
     def steer(n, carry):
-        d = n // XS
-        rel = n % XS
-        source = (here - d + 2 * TILES) % (2 * TILES)
-        sg = (x + XS - rel) % XS * 2 + source // TILES
-        line = sg * TILES + source % TILES
+        d = n >> 2
+        rel = n & (XS - 1)
+        source = (here - d) & (2 * TILES - 1)
+        line = (((x - rel) & (XS - 1)) * 2 + (source >> 6)) * TILES + (source & (TILES - 1))
 
         def both(i):
             row = half_row(steer_ref, line, i)
@@ -203,20 +214,14 @@
         left[COLS : 2 * COLS, at] = im
         return carry
 
-    lax.fori_loop(0, SLOTS, steer, 0)
-    pl.semaphore_wait(barrier, SLOTS + STEPS - 1)
-    for d in range(1, STEPS):
-        table_copy(d).start()
 
     def chunk(j, px, ph):
-        half = jnp.where(j < 2, 1 - ph, ph)
-        return px * 4 + half * 2 + j % 2
+        return px * 4 + (ph ^ 1 ^ (j >> 1)) * 2 + (j & 1)
 
     def send(j, n):
         pt, pg, ph = place(n, 1)
-        d = n // XS
         return pltpu.make_async_remote_copy(
-            src_ref=prof.at[d * ROW_BLOCKS + chunk(j, pg // 2, ph)],
+            src_ref=prof.at[(n >> 2) * ROW_BLOCKS + chunk(j, pg >> 1, ph)],
             dst_ref=held.at[j, pl.ds(pl.multiple_of(n * WIDE, WIDE), WIDE)],
             send_sem=ssem.at[j, n],
             recv_sem=rsem.at[j, n],
@@ -225,7 +230,7 @@
         )
 
     def distance(i, carry):
-        d = (STEPS - i) % STEPS
+        d = (STEPS - i) & (STEPS - 1)
 
         @pl.when(d > 0)
         def _():
@@ -237,25 +242,43 @@
 
         lax.fori_loop(0, PULSES // 16, part, 0)
 
-        def early(m, c):
-            n = d * XS + m % XS
-
-            @pl.when(n > 0)
-            def _():
-                send(m // XS, n).start()
-
+        @pl.when(d == 0)
+        def _():
+            pl.semaphore_wait(barrier, SLOTS + STEPS)
+            for b in range(1, STEPS):
+                table_copy(b).start()
+
+        def early(j, c):
+            for rel in range(XS):
+                n = d * XS + rel
+                if rel == 0:
+
+                    @pl.when(d > 0)
+                    def _():
+                        send(j, n).start()
+
+                else:
+                    send(j, n).start()
             return c
 
-        lax.fori_loop(0, 2 * XS, early, 0)
+        lax.fori_loop(0, 2, early, 0)
         return carry
 
     lax.fori_loop(0, STEPS, distance, 0)
 
-    def late(i, carry):
-        send(2 + i // (SLOTS - 1), i % (SLOTS - 1) + 1).start()
-        return carry
-
-    lax.fori_loop(0, 2 * (SLOTS - 1), late, 0)
+    def late(n, carry):
+        send(2, n).start()
+        send(3, n).start()
+        return carry
+
+    def early_drain(n, carry):
+        send(0, n).wait_send()
+        send(1, n).wait_send()
+        return carry
+
+    lax.fori_loop(0, SLOTS, steer, 0)
+    lax.fori_loop(1, SLOTS, early_drain, 0)
+    lax.fori_loop(1, SLOTS, late, 0)
 
     def take(j, carry):
         held[j, 0:WIDE, :] = prof[chunk(j, x, zh)]
@@ -271,19 +294,30 @@
         lax.fori_loop(1, SLOTS, one, 0)
         return jnp.dot(left[...], held[j], preferred_element_type=jnp.float32)
 
-    def across(j):
+    y = (t >> 1) & 3
+
+    def leg(j, k, second):
+        up = k < plus(y)
+        rows = pl.ds(pl.multiple_of(k * QROWS, QROWS), QROWS)
         return pltpu.make_async_remote_copy(
-            src_ref=zsend.at[j],
-            dst_ref=zheld.at[j],
-            send_sem=zssem.at[j],
-            recv_sem=zrsem.at[j],
-            device_id=(t, x * 2 + 1 - zh),
+            src_ref=(relay if second else zsend).at[j, rows],
+            dst_ref=(zheld if second else relay).at[j, rows],
+            send_sem=zssem.at[second, j, k],
+            recv_sem=zrsem.at[second, j, k],
+            device_id=along(jnp.where(up, LEG, -LEG)),
             device_id_type=MESH,
         )
 
     def far(j, carry):
         zsend[j] = arrived(j).astype(jnp.bfloat16)
-        across(j).start()
+        for k in range(QUARTERS):
+            leg(j, k, 0).start()
+        return carry
+
+    def forward(j, carry):
+        for k in range(QUARTERS):
+            leg(j, k, 0).wait_recv()
+            leg(j, k, 1).start()
         return carry
 
     def near(j, carry):
@@ -291,25 +325,37 @@
         return carry
 
     def finish(j, carry):
-        across(j).wait_recv()
-        total = (own[j] + zheld[j].astype(jnp.float32)) * scale
-        rows = pl.ds(pl.multiple_of(j * LANES, LANES), LANES)
-        out_ref[0, rows, :] = total[0:COLS].T
-        out_ref[1, rows, :] = total[COLS : 2 * COLS].T
-        return carry
-
-    def drain(i, carry):
-        send(i // (SLOTS - 1), i % (SLOTS - 1) + 1).wait_send()
+        for k in range(QUARTERS):
+            leg(j, k, 1).wait_recv()
+        out_ref[j] = (own[j] + zheld[j].astype(jnp.float32)) * scale
+        return carry
+
+    def late_drain(n, carry):
+        send(2, n).wait_send()
+        send(3, n).wait_send()
         return carry
 
     lax.fori_loop(0, 2, far, 0)
+    lax.fori_loop(0, 2, forward, 0)
     lax.fori_loop(0, 2, near, 0)
     lax.fori_loop(0, 2, finish, 0)
-    lax.fori_loop(0, PIECES * (SLOTS - 1), drain, 0)
+    lax.fori_loop(1, SLOTS, late_drain, 0)
     for d in range(1, STEPS):
         table_copy(d).wait_send()
-    across(0).wait_send()
-    across(1).wait_send()
+    for j in range(2):
+        for k in range(QUARTERS):
+            leg(j, k, 0).wait_send()
+            leg(j, k, 1).wait_send()
+
+
+def plus(y):
+    return jnp.where(y == 3, 2, 4)
+
+
+def turn_kernel(in_ref, out_ref):
+    for j in range(2):
+        for i in range(2):
+            out_ref[i, j * LANES : (j + 1) * LANES, :] = in_ref[j, i * COLS : (i + 1) * COLS].T
 
 
 def per_device(echoes, offsets, phase_index, steering, kernels):
@@ -317,9 +363,9 @@
     vmem = pl.BlockSpec(memory_space=pltpu.VMEM)
     rows = jnp.transpose(echoes, (1, 0, 2)).reshape(WIDE, echoes.shape[2])
     dma = pltpu.SemaphoreType.DMA
-    return pl.pallas_call(
+    total = pl.pallas_call(
         functools.partial(strip_kernel, scale),
-        out_shape=jax.ShapeDtypeStruct((2, COLS, COLS), jnp.float32),
+        out_shape=jax.ShapeDtypeStruct((2, 2 * COLS, LANES), jnp.float32),
         in_specs=[vmem] * 5,
         out_specs=vmem,
         scratch_shapes=[
@@ -331,16 +377,23 @@
             pltpu.VMEM((2 * COLS, SLOTS * WIDE), jnp.bfloat16),
             pltpu.VMEM((2, 2 * COLS, LANES), jnp.bfloat16),
             pltpu.VMEM((2, 2 * COLS, LANES), jnp.bfloat16),
+            pltpu.VMEM((2, 2 * COLS, LANES), jnp.bfloat16),
             pltpu.VMEM((2, 2 * COLS, LANES), jnp.float32),
             dma((STEPS,)),
             dma((STEPS,)),
             dma((PIECES, SLOTS)),
             dma((PIECES, SLOTS)),
-            dma((2,)),
-            dma((2,)),
+            dma((2, 2, QUARTERS)),
+            dma((2, 2, QUARTERS)),
         ],
         compiler_params=pltpu.CompilerParams(collective_id=0, has_side_effects=True),
-    )(rows, offsets, phase_index, steering, kernels)
+    )(rows, offsets, phase_index, steering, kernels.T)
+    return pl.pallas_call(
+        turn_kernel,
+        out_shape=jax.ShapeDtypeStruct((2, COLS, COLS), jnp.float32),
+        in_specs=[vmem],
+        out_specs=vmem,
+    )(total)
 
 
 def solution(mesh):

time: 91.8 us -> 81.9 us (0.89)
  the two profiles are of different devices: /device:TPU:10 before, /device:TPU:29 now
where the time goes in v3:
time: 81.9 us; the launch traced here: 81.7 us
  Pallas kernels  78.9 us (96%)
  local copies, waits for them, and re-layouts  2.79 us (3%)
    pallas_call x1, Pallas kernels, per_device(): pl.pallas_call(functools.partial(strip_kernel, scale), out_shape=jax.Shap...  76.8 us
    transpose x1, local copies, waits for them, and re-layouts, per_device(): rows = jnp.transpose(echoes, (1, 0, 2)).reshape(WIDE, echoes.shape[2])  2.79 us
    pallas_call x1, Pallas kernels, per_device(): pl.pallas_call(turn_kernel, out_shape=jax.ShapeDtypeStruct((2, COLS, COLS...  2.04 us

profile of v3, /device:TPU:29, one launch (start us, length us, event | category | flops | bytes accessed | tf_op | source)
XLA Modules:
  0.0 81.7 jit_solution(14923476697701153234)
XLA Ops:
  0.0 2.8 %copy.6 = bf16[2,64,4096]{2,1,0:T(8,128)(2,1)} copy(bf16[2,64,4096]{2,0,1:T(2,128)(2,1)} %bitcast.4) | data formatting | bytes 2097152 | tf_op jit(solution)/shard_map/transpose | solution.py:364
  2.8 76.8 %shard_map.55.in_ref = f32[2,512,128]{2,1,0:T(8,128)} custom-call(bf16[128,4096]{1,0:T(8,128)(2,1)} %bitcast.3, s32[1,4096]{1,0:T(1,128)} %offs_ref.1, s32[1,4096]{1,0:T(1,128)} %phase_ref.1, f32[2,1,32768]{2,1,0:T(1,128)} %steer_ref.1, f32[8,16]{1,0:T(8,128)} %bitcast.5), custom_call_target="tpu_custom_call" | custom-call | tf_op jit(solution)/shard_map/pallas_call | solution.py:366
  79.6 2.0 %shard_map.56 = f32[2,256,256]{2,1,0:T(8,128)} custom-call(f32[2,512,128]{2,1,0:T(8,128)} %shard_map.55.in_ref), custom_call_target="tpu_custom_call" | custom-call | tf_op jit(solution)/shard_map/pallas_call | solution.py:391

commit v4 on v3

--- a/solution.py
+++ b/solution.py
@@ -21,6 +21,8 @@
 LEG = 32
 QUARTERS = 8
 QROWS = 64
+BUSY = 3
+LENT = 6
 ROW_BLOCKS = 16
 BLOCKS_IN = 32
 SIN = (6.2831853, -41.3417004, 81.6051314, -76.7030154, 42.025927, -14.8998467, 3.23813751)
@@ -129,7 +131,7 @@
 
 def strip_kernel(
     scale, echo_ref, offs_ref, phase_ref, steer_ref, kern_ref, out_ref,
-    prof, tab, tsend, kpad, held, left, zsend, relay, zheld, own, tssem, trsem, ssem, rsem, zssem, zrsem,
+    prof, tab, tsend, kpad, held, left, zsend, relay, zheld, lent, own, tssem, trsem, ssem, rsem, zssem, zrsem, fssem, frsem,
 ):
     t = lax.axis_index("tile")
     g = lax.axis_index("pgroup")
@@ -155,8 +157,21 @@
         other = (here + by) & (2 * TILES - 1)
         return other & (TILES - 1), x * 2 + (other >> 6)
 
+    y = (t >> 1) & 3
     for by in (-LEG, LEG):
         pl.semaphore_signal(barrier, inc=1, device_id=along(by), device_id_type=MESH)
+
+    @pl.when(y == BUSY)
+    def _():
+        for column in range(BUSY):
+            pl.semaphore_signal(
+                barrier, inc=1, device_id=along(LEG + (column - BUSY) * 2), device_id_type=MESH
+            )
+
+    @pl.when(y != BUSY)
+    def _():
+        pl.semaphore_signal(barrier, inc=1, device_id=along(LEG + (BUSY - y) * 2), device_id_type=MESH)
+
     for d in range(1, STEPS):
         pl.semaphore_signal(barrier, inc=1, device_id=((t + d) & (TILES - 1), g), device_id_type=MESH)
 
@@ -244,7 +259,7 @@
 
         @pl.when(d == 0)
         def _():
-            pl.semaphore_wait(barrier, SLOTS + STEPS)
+            pl.semaphore_wait(barrier, SLOTS + STEPS + jnp.where(y == BUSY, BUSY, 1))
             for b in range(1, STEPS):
                 table_copy(b).start()
 
@@ -294,30 +309,73 @@
         lax.fori_loop(1, SLOTS, one, 0)
         return jnp.dot(left[...], held[j], preferred_element_type=jnp.float32)
 
-    y = (t >> 1) & 3
+    def rows_of(k):
+        return pl.ds(pl.multiple_of(k * QROWS, QROWS), QROWS)
 
     def leg(j, k, second):
-        up = k < plus(y)
-        rows = pl.ds(pl.multiple_of(k * QROWS, QROWS), QROWS)
+        up = jnp.logical_and(k < QUARTERS // 2, y != BUSY)
         return pltpu.make_async_remote_copy(
-            src_ref=(relay if second else zsend).at[j, rows],
-            dst_ref=(zheld if second else relay).at[j, rows],
+            src_ref=(relay if second else zsend).at[j, rows_of(k)],
+            dst_ref=(zheld if second else relay).at[j, rows_of(k)],
             send_sem=zssem.at[second, j, k],
             recv_sem=zrsem.at[second, j, k],
             device_id=along(jnp.where(up, LEG, -LEG)),
             device_id_type=MESH,
         )
 
+    def lend(j, k):
+        return pltpu.make_async_remote_copy(
+            src_ref=zsend.at[j, rows_of(k)],
+            dst_ref=lent.at[j, k & 1],
+            send_sem=zssem.at[0, j, k],
+            recv_sem=frsem.at[j, k & 1],
+            device_id=along(-LEG + ((k >> 1) - BUSY) * 2),
+            device_id_type=MESH,
+        )
+
+    def give(j, i):
+        return pltpu.make_async_remote_copy(
+            src_ref=lent.at[j, i],
+            dst_ref=zheld.at[j, rows_of(2 * y + i)],
+            send_sem=fssem.at[j, i],
+            recv_sem=zrsem.at[1, j, 2 * y + i],
+            device_id=along(-LEG + (BUSY - y) * 2),
+            device_id_type=MESH,
+        )
+
     def far(j, carry):
         zsend[j] = arrived(j).astype(jnp.bfloat16)
-        for k in range(QUARTERS):
+
+        @pl.when(y == BUSY)
+        def _():
+            for k in range(LENT):
+                lend(j, k).start()
+
+        @pl.when(y != BUSY)
+        def _():
+            for k in range(LENT):
+                leg(j, k, 0).start()
+
+        for k in range(LENT, QUARTERS):
             leg(j, k, 0).start()
         return carry
 
     def forward(j, carry):
-        for k in range(QUARTERS):
+        def on(k):
             leg(j, k, 0).wait_recv()
             leg(j, k, 1).start()
+
+        for k in range(LENT, QUARTERS):
+            on(k)
+
+        @pl.when(y != BUSY)
+        def _():
+            for k in range(LENT):
+                on(k)
+            for i in range(2):
+                lend(j, i).wait_recv()
+                give(j, i).start()
+
         return carry
 
     def near(j, carry):
@@ -345,11 +403,15 @@
     for j in range(2):
         for k in range(QUARTERS):
             leg(j, k, 0).wait_send()
+        for k in range(LENT, QUARTERS):
             leg(j, k, 1).wait_send()
 
-
-def plus(y):
-    return jnp.where(y == 3, 2, 4)
+        @pl.when(y != BUSY)
+        def _():
+            for k in range(LENT):
+                leg(j, k, 1).wait_send()
+            for i in range(2):
+                give(j, i).wait_send()
 
 
 def turn_kernel(in_ref, out_ref):
@@ -378,6 +440,7 @@
             pltpu.VMEM((2, 2 * COLS, LANES), jnp.bfloat16),
             pltpu.VMEM((2, 2 * COLS, LANES), jnp.bfloat16),
             pltpu.VMEM((2, 2 * COLS, LANES), jnp.bfloat16),
+            pltpu.VMEM((2, 2, QROWS, LANES), jnp.bfloat16),
             pltpu.VMEM((2, 2 * COLS, LANES), jnp.float32),
             dma((STEPS,)),
             dma((STEPS,)),
@@ -385,6 +448,8 @@
             dma((PIECES, SLOTS)),
             dma((2, 2, QUARTERS)),
             dma((2, 2, QUARTERS)),
+            dma((2, 2)),
+            dma((2, 2)),
         ],
         compiler_params=pltpu.CompilerParams(collective_id=0, has_side_effects=True),
     )(rows, offsets, phase_index, steering, kernels.T)

time: 81.9 us -> 78.4 us (0.957)
  the two profiles are of different devices: /device:TPU:29 before, /device:TPU:121 now
where the time goes in v4:
time: 78.4 us; the launch traced here: 78.2 us
  Pallas kernels  75.4 us (96%)
  local copies, waits for them, and re-layouts  2.79 us (4%)
    pallas_call x1, Pallas kernels, per_device(): pl.pallas_call(functools.partial(strip_kernel, scale), out_shape=jax.Shap...  73.4 us
    transpose x1, local copies, waits for them, and re-layouts, per_device(): rows = jnp.transpose(echoes, (1, 0, 2)).reshape(WIDE, echoes.shape[2])  2.79 us
    pallas_call x1, Pallas kernels, per_device(): pl.pallas_call(turn_kernel, out_shape=jax.ShapeDtypeStruct((2, COLS, COLS...  2.04 us

profile of v4, /device:TPU:121, one launch (start us, length us, event | category | flops | bytes accessed | tf_op | source)
XLA Modules:
  0.0 78.2 jit_solution(2361745244734371531)
XLA Ops:
  0.0 2.8 %copy.6 = bf16[2,64,4096]{2,1,0:T(8,128)(2,1)} copy(bf16[2,64,4096]{2,0,1:T(2,128)(2,1)} %bitcast.4) | data formatting | bytes 2097152 | tf_op jit(solution)/shard_map/transpose | solution.py:426
  2.8 73.4 %shard_map.55.in_ref = f32[2,512,128]{2,1,0:T(8,128)} custom-call(bf16[128,4096]{1,0:T(8,128)(2,1)} %bitcast.3, s32[1,4096]{1,0:T(1,128)} %offs_ref.1, s32[1,4096]{1,0:T(1,128)} %phase_ref.1, f32[2,1,32768]{2,1,0:T(1,128)} %steer_ref.1, f32[8,16]{1,0:T(8,128)} %bitcast.5), custom_call_target="tpu_custom_call" | custom-call | tf_op jit(solution)/shard_map/pallas_call | solution.py:428
  76.2 2.0 %shard_map.56 = f32[2,256,256]{2,1,0:T(8,128)} custom-call(f32[2,512,128]{2,1,0:T(8,128)} %shard_map.55.in_ref), custom_call_target="tpu_custom_call" | custom-call | tf_op jit(solution)/shard_map/pallas_call | solution.py:456

commit v5 on v4

--- a/solution.py
+++ b/solution.py
@@ -244,8 +244,10 @@
             device_id_type=MESH,
         )
 
+    first_slots = jnp.where(t > TILES - STEPS, SLOTS, SLOTS // 2)
+
     def distance(i, carry):
-        d = (STEPS - i) & (STEPS - 1)
+        d = i
 
         @pl.when(d > 0)
         def _():
@@ -263,23 +265,24 @@
             for b in range(1, STEPS):
                 table_copy(b).start()
 
-        def early(j, c):
-            for rel in range(XS):
-                n = d * XS + rel
-                if rel == 0:
-
-                    @pl.when(d > 0)
-                    def _():
-                        send(j, n).start()
-
-                else:
-                    send(j, n).start()
-            return c
-
-        lax.fori_loop(0, 2, early, 0)
+        @pl.when(d > 0)
+        def _():
+            send(0, d * XS).start()
+
+        for rel in range(1, XS):
+            send(0, d * XS + rel).start()
+
+        @pl.when(d == 0)
+        def _():
+            lax.fori_loop(0, first_slots, steer, 0)
+
         return carry
 
     lax.fori_loop(0, STEPS, distance, 0)
+
+    def second(n, carry):
+        send(1, n).start()
+        return carry
 
     def late(n, carry):
         send(2, n).start()
@@ -291,9 +294,8 @@
         send(1, n).wait_send()
         return carry
 
-    lax.fori_loop(0, SLOTS, steer, 0)
-    lax.fori_loop(1, SLOTS, early_drain, 0)
-    lax.fori_loop(1, SLOTS, late, 0)
+    lax.fori_loop(1, SLOTS, second, 0)
+    lax.fori_loop(first_slots, SLOTS, steer, 0)
 
     def take(j, carry):
         held[j, 0:WIDE, :] = prof[chunk(j, x, zh)]
@@ -393,7 +395,10 @@
         send(3, n).wait_send()
         return carry
 
-    lax.fori_loop(0, 2, far, 0)
+    far(0, 0)
+    lax.fori_loop(1, SLOTS, early_drain, 0)
+    lax.fori_loop(1, SLOTS, late, 0)
+    far(1, 0)
     lax.fori_loop(0, 2, forward, 0)
     lax.fori_loop(0, 2, near, 0)
     lax.fori_loop(0, 2, finish, 0)

time: 78.4 us -> 77 us (0.982)
  the two profiles are of different devices: /device:TPU:121 before, /device:TPU:31 now
where the time goes in v5:
time: 77 us; the launch traced here: 76.8 us
  Pallas kernels  74 us (96%)
  local copies, waits for them, and re-layouts  2.79 us (4%)
    pallas_call x1, Pallas kernels, per_device(): pl.pallas_call(functools.partial(strip_kernel, scale), out_shape=jax.Shap...  71.9 us
    transpose x1, local copies, waits for them, and re-layouts, per_device(): rows = jnp.transpose(echoes, (1, 0, 2)).reshape(WIDE, echoes.shape[2])  2.79 us
    pallas_call x1, Pallas kernels, per_device(): pl.pallas_call(turn_kernel, out_shape=jax.ShapeDtypeStruct((2, COLS, COLS...  2.04 us

profile of v5, /device:TPU:31, one launch (start us, length us, event | category | flops | bytes accessed | tf_op | source)
XLA Modules:
  0.0 76.8 jit_solution(370396326978427946)
XLA Ops:
  0.0 2.8 %copy.6 = bf16[2,64,4096]{2,1,0:T(8,128)(2,1)} copy(bf16[2,64,4096]{2,0,1:T(2,128)(2,1)} %bitcast.4) | data formatting | bytes 2097152 | tf_op jit(solution)/shard_map/transpose | solution.py:431
  2.8 71.9 %shard_map.55.in_ref = f32[2,512,128]{2,1,0:T(8,128)} custom-call(bf16[128,4096]{1,0:T(8,128)(2,1)} %bitcast.3, s32[1,4096]{1,0:T(1,128)} %offs_ref.1, s32[1,4096]{1,0:T(1,128)} %phase_ref.1, f32[2,1,32768]{2,1,0:T(1,128)} %steer_ref.1, f32[8,16]{1,0:T(8,128)} %bitcast.5), custom_call_target="tpu_custom_call" | custom-call | tf_op jit(solution)/shard_map/pallas_call | solution.py:433
  74.7 2.0 %shard_map.56 = f32[2,256,256]{2,1,0:T(8,128)} custom-call(f32[2,512,128]{2,1,0:T(8,128)} %shard_map.55.in_ref), custom_call_target="tpu_custom_call" | custom-call | tf_op jit(solution)/shard_map/pallas_call | solution.py:461

commit v6 on v5

--- a/solution.py
+++ b/solution.py
@@ -456,13 +456,16 @@
             dma((2, 2)),
             dma((2, 2)),
         ],
-        compiler_params=pltpu.CompilerParams(collective_id=0, has_side_effects=True),
+        compiler_params=pltpu.CompilerParams(
+            collective_id=0, has_side_effects=True, vmem_limit_bytes=24 * 1024 * 1024
+        ),
     )(rows, offsets, phase_index, steering, kernels.T)
     return pl.pallas_call(
         turn_kernel,
         out_shape=jax.ShapeDtypeStruct((2, COLS, COLS), jnp.float32),
         in_specs=[vmem],
         out_specs=vmem,
+        compiler_params=pltpu.CompilerParams(vmem_limit_bytes=8 * 1024 * 1024),
     )(total)
 
 

time: 77 us -> 72.2 us (0.938)
  the two profiles are of different devices: /device:TPU:31 before, /device:TPU:10 now
where the time goes in v6:
time: 72.2 us; the launch traced here: 72 us
  Pallas kernels  70.1 us (97%)
  local copies, waits for them, and re-layouts  1.86 us (3%)
    pallas_call x1, Pallas kernels, per_device(): pl.pallas_call(functools.partial(strip_kernel, scale), out_shape=jax.Shap...  69.1 us
    transpose x1, local copies, waits for them, and re-layouts, per_device(): rows = jnp.transpose(echoes, (1, 0, 2)).reshape(WIDE, echoes.shape[2])  1.85 us

profile of v6, /device:TPU:10, one launch (start us, length us, event | category | flops | bytes accessed | tf_op | source)
XLA Modules:
  0.0 72.0 jit_solution(2613920110562153684)
XLA Ops:
  0.0 0.0 copy-start
  0.0 0.0 copy-start.1
  0.0 0.0 copy-start.2
  0.0 0.0 copy-start.3
  0.0 1.8 %copy.6 = bf16[2,64,4096]{2,1,0:T(8,128)(2,1)S(1)} copy(bf16[2,64,4096]{2,0,1:T(2,128)(2,1)} %bitcast.5) | data formatting | bytes 2097152 | tf_op jit(solution)/shard_map/transpose | solution.py:431
  1.9 0.0 copy-done
  1.9 0.0 copy-done.1
  1.9 0.0 copy-done.2
  1.9 0.0 copy-done.3
  1.9 69.1 %shard_map.55.in_ref = f32[2,512,128]{2,1,0:T(8,128)S(1)} custom-call(bf16[128,4096]{1,0:T(8,128)(2,1)S(1)} %bitcast.3, s32[1,4096]{1,0:T(1,128)S(1)} %copy-done.1, s32[1,4096]{1,0:T(1,128)S(1)} %copy-done.2, f32[2,1,32768]{2,1,0:T(1,128)S(1)} %copy-done, f32[8,16]{1,0:T(8,128)S(1)} %bitcast.4), custom_call_target="tpu_custom_call" | custom-call | tf_op jit(solution)/shard_map/pallas_call | solution.py:433
  71.0 1.0 %shard_map.56 = f32[2,256,256]{2,1,0:T(8,128)} custom-call(f32[2,512,128]{2,1,0:T(8,128)S(1)} %shard_map.55.in_ref), custom_call_target="tpu_custom_call" | custom-call | tf_op jit(solution)/shard_map/pallas_call | solution.py:463
Async XLA Ops:
  0.0 1.9 %copy-start = (f32[2,1,32768]{2,1,0:T(1,128)S(1)}, f32[2,1,32768]{2,1,0:T(1,128)}, u32[]{:S(2)}) copy-start(f32[2,1,32768]{2,1,0:T(1,128)} %steer_ref.1) | copy-start | bytes 786436
  0.0 1.9 %copy-start.1 = (s32[1,4096]{1,0:T(1,128)S(1)}, s32[1,4096]{1,0:T(1,128)}, u32[]{:S(2)}) copy-start(s32[1,4096]{1,0:T(1,128)} %offs_ref.1) | copy-start | bytes 49156
  0.0 1.9 %copy-start.2 = (s32[1,4096]{1,0:T(1,128)S(1)}, s32[1,4096]{1,0:T(1,128)}, u32[]{:S(2)}) copy-start(s32[1,4096]{1,0:T(1,128)} %phase_ref.1) | copy-start | bytes 49156
  0.0 1.9 %copy-start.3 = (f32[16,8]{0,1:T(8,128)S(1)}, f32[16,8]{0,1:T(8,128)}, u32[]{:S(2)}) copy-start(f32[16,8]{0,1:T(8,128)} %param.9) | copy-start | bytes 1540
